TPU v7x, 32 devices: a whole 2x2x4 slice. The times are simulated.
32 devices in a mesh: patch: 2 (over y), exp: 4 (over z), tile: 2 (over x), band: 2 (over core).
Axes of the slice: x: 2, y: 2, z: 4, core: 2. Of those that a mesh axis runs over, the one named last changes fastest.
Arguments:
- images: bfloat16 [4, 2, 64, 128, 128], P(('patch', 'band'), 'tile', 'exp'), parts along dimension 0, may hold values from -6 to 6
- mask_bits: int32 [4, 2, 64, 128, 128], P(('patch', 'band'), 'tile', 'exp'), parts along dimension 0, may hold values from 0 to 7
- inv_var: float32 [4, 2, 64], P(('patch', 'band'), 'tile', 'exp'), parts along dimension 0, may hold values from 0.5 to 4
- routes: int32 [4, 2, 64, 1], P(('patch', 'band'), 'tile', 'exp'), parts along dimension 0, may hold values from 0 to 3; in each aligned block of 16 rows (0 to 15, 16 to 31, ..., all dimensions but the last counted through in order) at most 8 rows name the same one
- block_slot: int32 [4, 2, 64], P(('patch', 'band'), 'tile', 'exp'), parts along dimension 0, may hold values from 0 to 7
- kernel_index: int32 [4, 2, 64], P(('patch', 'band'), 'tile', 'exp'), parts along dimension 0, may hold values from 0 to 63
- coefficients: float32 [64, 3], replicated, may hold values from -4 to 4
Outputs:
- coadd: float32 [4, 512, 2048], P(('patch', 'band'), 'tile', 'exp'), parts along dimension 0
- detection: float32 [1024, 2048], P(('patch', 'tile'), 'exp'), parts along dimension 0
There are 2 independent parts, one for each index of `patch`. A program takes and returns all parts, laid end to end along the dimension named above; an argument that names none is the same for every part. Nothing has to cross between parts.
Inputs may be any that keep to these rules, and one draw needn't show every extreme that they name: Among the 16 sub-blocks of one device for one band and strip (an aligned block of routes), no tile column is named more than 8 times, and some tile column is named exactly 8 times.
All inputs are finite; a program needn't handle non-finite values.
Results may differ from a plain program's by a relative error of at most 0.0039.
Values may be sent and summed in bfloat16 or wider, within the bound.
A program may use at most 128 MiB of HBM per device.

v0:
```python
import jax
import jax.numpy as jnp
from jax import lax
from jax.sharding import PartitionSpec as P

BLOCK = 128
TAPS = 41
BLOCK_ROWS = 2
BLOCK_COLS = 4
kernel_sigmas = (1.0, 2.5, 6.0)


def extended(block, sides, width):
    for axis, dim in sides:
        count = lax.axis_size(axis)
        forward = [(i, i + 1) for i in range(count - 1)]
        backward = [(target, source) for source, target in forward]
        low = lax.ppermute(
            lax.slice_in_dim(block, block.shape[dim] - width, None, axis=dim), axis, forward
        )
        high = lax.ppermute(lax.slice_in_dim(block, 0, width, axis=dim), axis, backward)
        block = jnp.concatenate([low, block, high], axis=dim)
    return block


def usable_share(bits):
    flagged = jnp.bitwise_and(bits, 6) == 6
    suspect = jnp.bitwise_and(bits, 1).astype(jnp.float32)
    return jnp.where(flagged, 0.0, 1.0 - 0.5 * suspect)


def band_matrix(length, half_span):
    rows_here = jnp.arange(length + 2 * half_span, dtype=jnp.int32)[:, None]
    cols_here = jnp.arange(length, dtype=jnp.int32)[None, :]
    offset = (rows_here - cols_here - half_span).astype(jnp.float32)
    inside = jnp.abs(offset) <= half_span
    taps_axis = jnp.arange(-half_span, half_span + 1).astype(jnp.float32)
    result = []
    for spread in kernel_sigmas:
        norm_sum = jnp.sum(jnp.exp(-taps_axis * taps_axis / (2.0 * spread * spread)))
        result.append(
            jnp.where(inside, jnp.exp(-offset * offset / (2.0 * spread * spread)), 0.0) / norm_sum
        )
    return jnp.stack(result)


def local(images, mask_bits, inv_var, routes, block_slot, kernel_index, coefficients):
    peer_count = lax.axis_size("exp")
    held_count = images.shape[2]
    capacity = max(2, 2 * held_count // peer_count)
    slot_count = peer_count * capacity
    pixels = BLOCK * BLOCK
    tile_blocks = BLOCK_ROWS * BLOCK_COLS
    coef_count = coefficients.shape[0]
    usable = usable_share(mask_bits[0, 0])
    inverse = inv_var[0, 0][:, None, None]
    weight = (usable * inverse).astype(jnp.bfloat16).reshape(held_count, pixels)
    weighted = (
        (usable * inverse * images[0, 0].astype(jnp.float32))
        .astype(jnp.bfloat16)
        .reshape(held_count, pixels)
    )
    target = routes[0, 0, :, 0]
    ordinal = jnp.arange(held_count, dtype=jnp.int32)
    same_target = target[:, None] == target[None, :]
    earlier = jnp.sum(
        (same_target & (ordinal[None, :] < ordinal[:, None])).astype(jnp.int32), axis=1
    )
    position = target * capacity + earlier
    placed = jnp.arange(slot_count, dtype=jnp.int32)[:, None] == position[None, :]
    placed_int = placed.astype(jnp.int32)
    slot_block = jnp.sum(placed_int * (block_slot[0, 0] + 1)[None, :], axis=1) - 1
    slot_kernel = jnp.sum(placed_int * kernel_index[0, 0][None, :], axis=1)
    labels = jnp.stack([slot_block, slot_kernel], axis=1).reshape(peer_count, capacity, 2)
    placed_half = placed.astype(jnp.bfloat16)
    send_weight = (
        jnp.dot(placed_half, weight, preferred_element_type=jnp.float32)
        .astype(jnp.bfloat16)
        .reshape(peer_count, capacity, pixels)
    )
    block_ids = jnp.arange(tile_blocks, dtype=jnp.int32)[:, None]
    send_weighted = (
        jnp.dot(placed_half, weighted, preferred_element_type=jnp.float32)
        .astype(jnp.bfloat16)
        .reshape(peer_count, capacity, pixels)
    )
    got_weighted, got_weight, got_labels = (
        lax.all_to_all(send_weighted, "exp", split_axis=0, concat_axis=0, tiled=True),
        lax.all_to_all(send_weight, "exp", split_axis=0, concat_axis=0, tiled=True),
        lax.all_to_all(labels, "exp", split_axis=0, concat_axis=0, tiled=True),
    )
    got_labels = got_labels.reshape(slot_count, 2)
    into_block = block_ids == got_labels[:, 0][None, :]
    kernel_pick = (
        got_labels[:, 1][:, None] == jnp.arange(coef_count, dtype=jnp.int32)[None, :]
    ).astype(jnp.float32)
    slot_mix = jnp.dot(kernel_pick, coefficients, precision=lax.Precision.HIGHEST)
    mixing = slot_mix.T[:, None, :] * into_block.astype(jnp.float32)[None, :, :]
    basis_sum = jnp.einsum(
        "kbp,px->kbx",
        mixing,
        got_weighted.reshape(slot_count, pixels).astype(jnp.float32),
        precision=lax.Precision.HIGHEST,
    )
    depth_sum = jnp.dot(
        into_block.astype(jnp.bfloat16),
        got_weight.reshape(slot_count, pixels),
        preferred_element_type=jnp.float32,
    )
    tile_rows = BLOCK_ROWS * BLOCK
    tile_cols = BLOCK_COLS * BLOCK
    basis_tile = (
        basis_sum.reshape(3, BLOCK_ROWS, BLOCK_COLS, BLOCK, BLOCK)
        .transpose(0, 1, 3, 2, 4)
        .reshape(3, tile_rows, tile_cols)
    )
    depth_tile = (
        depth_sum.reshape(BLOCK_ROWS, BLOCK_COLS, BLOCK, BLOCK)
        .transpose(0, 2, 1, 3)
        .reshape(tile_rows, tile_cols)
    )
    half_span = TAPS // 2
    column_mix = band_matrix(tile_cols, half_span)
    row_mix = band_matrix(tile_rows, half_span).transpose(0, 2, 1)
    framed = extended(basis_tile, (("exp", 2), ("tile", 1)), half_span)
    across = jnp.einsum("kyp,kpc->kyc", framed, column_mix, precision=lax.Precision.HIGHEST)
    matched = jnp.einsum("kry,kyc->rc", row_mix, across, precision=lax.Precision.HIGHEST)
    denominator = 1.0 + depth_tile
    coadded = matched / denominator
    detection = lax.psum(coadded * coadded * denominator, "band")
    return (coadded[None], detection)


def solution(mesh):
    return jax.shard_map(
        local,
        mesh=mesh,
        in_specs=(
            P(("patch", "band"), "tile", "exp", None, None),
            P(("patch", "band"), "tile", "exp", None, None),
            P(("patch", "band"), "tile", "exp"),
            P(("patch", "band"), "tile", "exp", None),
            P(("patch", "band"), "tile", "exp"),
            P(("patch", "band"), "tile", "exp"),
            P(),
        ),
        out_specs=(P(("patch", "band"), "tile", "exp"), P(("patch", "tile"), "exp")),
        check_vma=False,
    )
```

profile of v0, /device:TPU:0, one launch (start us, length us, event | category | flops | bytes accessed | tf_op | source)
XLA Modules:
  0.0 137.2 jit_solution(16599511198700164798)
XLA Ops:
  7.2 0.0 copy-start
  7.2 0.7 add_bitcast_fusion
  7.9 0.9 convert_reduce_fusion
  8.8 0.7 multiply_add_fusion.1
  9.5 0.7 select_reduce_fusion.1
  10.2 0.1 stack.9
  10.3 0.1 sub.118
  10.4 0.6 copy.15
  11.0 6.3 %all-to-all-start = ((s32[4,8,2]{1,2,0:T(2,128)}), s32[4,8,2]{1,2,0:T(2,128)S(1)}, u32[]{:S(2)}, u32[]{:S(2)}) async-start(s32[4,8,2]{1,2,0:T(2,128)} %copy.15), calls=%async_computation | async-start | bytes 8192 | tf_op jit(solution)/shard_map/all_to_all | solution.py:90
  17.4 1.5 %subtract_select_fusion = f32[1,1,16,128,128]{4,3,2,1,0:T(8,128)S(1)} fusion(s32[1,1,16,128,128]{4,3,2,1,0:T(8,128)} %param.8), kind=kLoop, calls=%fused_computation.36 | loop fusion | flops 1835008 | bytes 2097152 | tf_op jit(solution)/shard_map/jit(_where)/select_n | solution.py:29
  18.8 0.0 copy-start.7
  18.8 0.1 convert.1
  18.9 0.5 copy-done.7
  19.5 2.4 %fusion = bf16[4,8,16384]{2,1,0:T(8,128)(2,1)} fusion(f32[2,8,128,128]{3,2,1,0:T(8,128)S(1)} %convert.1, f32[2,8,128,128]{3,2,1,0:T(8,128)S(1)} %bitcast.88, f32[16]{0:T(128)S(1)} %bitcast.95, s32[16]{0:T(128)S(1)} %multiply_add_fusion.1), kind=kOutput, calls=%fused_computation.2 | convolution fusion | flops 18088448 | bytes 3145856 | tf_op jit(solution)/shard_map/dot_general | solution.py:83
  21.9 1.1 all-to-all-done
  22.9 4.0 %all-to-all-start.1 = ((bf16[4,8,16384]{2,1,0:T(8,128)(2,1)}), bf16[4,8,16384]{2,1,0:T(8,128)(2,1)S(1)}, u32[]{:S(2)}, u32[]{:S(2)}) async-start(bf16[4,8,16384]{2,1,0:T(8,128)(2,1)} %fusion), calls=%async_computation.1 | async-start | bytes 2097152 | tf_op jit(solution)/shard_map/all_to_all | solution.py:88
  27.0 0.6 exponential_reduce_fusion
  27.6 0.6 exponential_reduce_fusion.1
  28.2 0.6 exponential_reduce_fusion.2
  28.8 1.8 %fusion.1 = bf16[4,8,16384]{2,1,0:T(8,128)(2,1)} fusion(f32[2,8,128,128]{3,2,1,0:T(8,128)S(1)} %bitcast.89, f32[16]{0:T(128)S(1)} %bitcast.96, s32[16]{0:T(128)S(1)} %multiply_add_fusion.1), kind=kOutput, calls=%fused_computation.3 | convolution fusion | flops 17826304 | bytes 2097280 | tf_op jit(solution)/shard_map/dot_general | solution.py:77
  30.6 2.0 %select_divide_fusion.2 = f32[1,552,512]{2,1,0:T(8,128)} fusion(f32[]{:T(128)} %exponential_reduce_fusion.2), kind=kLoop, calls=%fused_computation.26 | loop fusion | flops 2826240 | bytes 1130500 | tf_op jit(solution)/shard_map/div | solution.py:42
  32.6 3.3 %select_divide_fusion = (f32[1,552,512]{2,1,0:T(8,128)}, f32[1,552,512]{2,1,0:T(8,128)}) fusion(f32[]{:T(128)} %exponential_reduce_fusion, f32[]{:T(128)} %exponential_reduce_fusion.1), kind=kLoop, calls=%fused_computation.24 | loop fusion | flops 3674112 | bytes 2261000 | tf_op jit(solution)/shard_map/div | solution.py:42
  36.0 16.2 %all-to-all-done.1 = bf16[4,8,16384]{2,1,0:T(8,128)(2,1)S(1)} async-done(((bf16[4,8,16384]{2,1,0:T(8,128)(2,1)}), bf16[4,8,16384]{2,1,0:T(8,128)(2,1)S(1)}, u32[]{:S(2)}, u32[]{:S(2)}) %all-to-all-start.1) | async-done | bytes 1048608 | tf_op jit(solution)/shard_map/all_to_all | solution.py:88
  52.1 4.3 %all-to-all-start.2 = ((bf16[4,8,16384]{2,1,0:T(8,128)(2,1)}), bf16[4,8,16384]{2,1,0:T(8,128)(2,1)}, u32[]{:S(2)}, u32[]{:S(2)}) async-start(bf16[4,8,16384]{2,1,0:T(8,128)(2,1)} %fusion.1), calls=%async_computation.2 | async-start | bytes 2097152 | tf_op jit(solution)/shard_map/all_to_all | solution.py:89
  56.4 0.0 all-reduce.2.cloned.1.call-start
  56.4 2.2 %select_divide_fusion.3 = (f32[1,296,256]{2,1,0:T(8,128)S(1)}, f32[1,296,256]{2,1,0:T(8,128)}) fusion(f32[]{:T(128)} %exponential_reduce_fusion, f32[]{:T(128)} %exponential_reduce_fusion.1), kind=kLoop, calls=%fused_computation.48 | loop fusion | flops 985088 | bytes 606216 | tf_op jit(solution)/shard_map/div | solution.py:42
  58.6 0.1 reshape.298
  58.7 0.2 convolution_bitcast_fusion.2
  58.9 0.1 compare_convert_fusion
  59.0 0.3 copy.27
  59.3 1.5 %convolution_bitcast_fusion = f32[3,2,128,4,128]{4,3,2,1,0:T(4,128)S(1)} fusion(bf16[128,128,32,1,1]{1,0,2,4,3:T(8,128)(2,1)S(1)} %bitcast.91, f32[2,4,32]{2,1,0:T(4,128)S(1)} %compare_convert_fusion, f32[3,32]{1,0:T(4,128)S(1)} %convolution_bitcast_fusion.2), kind=kOutput, calls=%fused_computation.20 | convolution fusion | flops 150995712 | bytes 2622848 | tf_op jit(solution)/shard_map/kbp,px->kbx/dot_general | solution.py:99
  60.8 0.6 reshape.301
  61.4 0.2 fusion.42
  61.6 1.3 collective-permute-start.1
  62.9 4.6 %collective-permute-start = (f32[3,256,20]{2,1,0:T(8,128)S(1)}, f32[3,256,20]{2,1,0:T(8,128)S(1)}, u32[]{:S(2)}, u32[]{:S(2)}) collective-permute-start(f32[3,256,20]{2,1,0:T(8,128)S(1)} %get-tuple-element.6), channel_id=1, source_target_pairs={{0,4},{4,8},{8,12},{1,5},{5,9},{9,13},{2,6},{6,10},{10,14},{3,7},{... | collective-permute-start | bytes 184328 | tf_op jit(solution)/shard_map/ppermute | solution.py:18
  67.5 0.7 select_divide_fusion.5
  68.2 15.4 %collective-permute-done.1 = f32[3,256,20]{2,1,0:T(8,128)S(1)} collective-permute-done((f32[3,256,20]{2,1,0:T(8,128)S(1)}, f32[3,256,20]{2,1,0:T(8,128)S(1)}, u32[]{:S(2)}, u32[]{:S(2)}) %collective-permute-start.1) | collective-permute-done | bytes 61472 | tf_op jit(solution)/shard_map/ppermute | solution.py:21
  83.6 0.0 collective-permute-done
  83.6 0.9 pad_maximum_fusion.2
  84.5 1.4 %collective-permute-start.3 = (f32[3,20,552]{2,1,0:T(8,128)}, f32[3,20,552]{2,1,0:T(8,128)}, u32[]{:S(2)}, u32[]{:S(2)}) collective-permute-start(f32[3,20,552]{2,1,0:T(8,128)} %get-tuple-element.5), channel_id=1, source_target_pairs={{2,0},{3,1},{6,4},{7,5},{10,8},{11,9},{14,12},{15,13},{18,16},{19,... | collective-permute-start | bytes 397448 | tf_op jit(solution)/shard_map/ppermute | solution.py:21
  85.9 5.9 %collective-permute-start.2 = (f32[3,20,552]{2,1,0:T(8,128)S(1)}, f32[3,20,552]{2,1,0:T(8,128)}, u32[]{:S(2)}, u32[]{:S(2)}) collective-permute-start(f32[3,20,552]{2,1,0:T(8,128)S(1)} %get-tuple-element.4), channel_id=1, source_target_pairs={{0,2},{1,3},{4,6},{5,7},{8,10},{9,11},{12,14},{13,15},{16,18},{17,... | collective-permute-start | bytes 397448 | tf_op jit(solution)/shard_map/ppermute | solution.py:18
  91.8 1.6 %convolution_add_fusion = f32[2,4,128,128]{3,1,2,0:T(4,128)S(1)} fusion(s32[32]{0:T(128)S(1)} %get-tuple-element.9, s32[2,4]{1,0:T(2,128)S(1)} %multiply_add_fusion, bf16[4,8,16384]{2,1,0:T(8,128)(2,1)} %all-to-all-done.2), kind=kOutput, calls=%fused_computation.22 | convolution fusion | flops 8519936 | bytes 1573024 | tf_op jit(solution)/shard_map/dot_general | solution.py:105
  93.4 0.7 collective-permute-done.2
  94.2 6.7 %fusion.2 = f32[3,296,512]{2,1,0:T(8,128)S(1)} fusion(f32[1,552,512]{2,1,0:T(8,128)} %get-tuple-element.12, f32[1,552,512]{2,1,0:T(8,128)} %get-tuple-element.13, f32[1,552,512]{2,1,0:T(8,128)S(1)} %copy-done.2, f32[3,20,552]{2,1,0:T(8,128)} %collective-permute-done.3, f32[3,256,20]{2,1,0:T(8,128)S(1)} %copy-done.5, f32[3,256,512]{2,1,0:T(8,128)S(1)} %reshape.301, ...), kind=kOutput, calls=%fused_computation.4 | convolution fusion | flops 3015297792 | bytes 7170816 | tf_op jit(solution)/shard_map/kyp,kpc->kyc/dot_general | solution.py:126
  100.8 2.9 %bitcast_multiply_fusion.2 = (f32[256,512]{1,0:T(8,128)}, f32[256,512]{1,0:T(8,128)}) fusion(f32[32,8,4,128]{3,2,1,0:T(4,128)S(1)} %bitcast.92, f32[3,296,512]{2,1,0:T(8,128)S(1)} %fusion.2, f32[1,296,256]{2,1,0:T(8,128)S(1)} %get-tuple-element.14, f32[1,296,256]{2,1,0:T(8,128)S(1)} %copy-done.1, f32[1,296,256]{2,1,0:T(8,128)S(1)} %select_divide_fusion.5), kind=kOutput, calls=%fused_computation.44 | convolution fusion | flops 1397551104 | bytes 4300800 | tf_op jit(solution)/shard_map/kry,kyc->rc/dot_general | solution.py:127
  103.8 0.0 all-reduce.2.cloned.1.call-update
  103.8 24.6 %all-reduce.2.cloned.1.call-done = f32[256,512]{1,0:T(8,128)} async-done(((f32[256,512]{1,0:T(8,128)}), f32[256,512]{1,0:T(8,128)}) %all-reduce.2.cloned.1.call-update) | async-done | bytes 524304 | tf_op jit(solution)/shard_map/psum | solution.py:130
  128.4 1.9 %copy.47 = f32[256,512]{1,0:T(8,128)} copy(f32[256,512]{1,0:T(8,128)} %all-reduce.2.cloned.1.call-done) | data formatting | bytes 1048576
  (20 shorter events, 0.1 us)
Async XLA Ops:
  7.2 51.6 %copy-start = (f32[64,3]{0,1:T(4,128)S(1)}, f32[64,3]{0,1:T(4,128)}, u32[]{:S(2)}) copy-start(f32[64,3]{0,1:T(4,128)} %param.13) | copy-start | bytes 2308
  7.2 11.7 %copy-start.3 = (bf16[1,1,16,128,128]{4,3,2,1,0:T(8,128)(2,1)S(1)}, bf16[1,1,16,128,128]{4,3,2,1,0:T(8,128)(2,1)}, u32[]{:S(2)}) copy-start(bf16[1,1,16,128,128]{4,3,2,1,0:T(8,128)(2,1)} %param.7) | copy-start | bytes 1572868
  11.0 11.9 %all-to-all-start = ((s32[4,8,2]{1,2,0:T(2,128)}), s32[4,8,2]{1,2,0:T(2,128)S(1)}, u32[]{:S(2)}, u32[]{:S(2)}) async-start(s32[4,8,2]{1,2,0:T(2,128)} %copy.15), calls=%async_computation | async-start | bytes 8192 | tf_op jit(solution)/shard_map/all_to_all | solution.py:90
  18.8 0.7 copy-start.7
  22.9 29.2 %all-to-all-start.1 = ((bf16[4,8,16384]{2,1,0:T(8,128)(2,1)}), bf16[4,8,16384]{2,1,0:T(8,128)(2,1)S(1)}, u32[]{:S(2)}, u32[]{:S(2)}) async-start(bf16[4,8,16384]{2,1,0:T(8,128)(2,1)} %fusion), calls=%async_computation.1 | async-start | bytes 2097152 | tf_op jit(solution)/shard_map/all_to_all | solution.py:88
  52.1 39.7 %all-to-all-start.2 = ((bf16[4,8,16384]{2,1,0:T(8,128)(2,1)}), bf16[4,8,16384]{2,1,0:T(8,128)(2,1)}, u32[]{:S(2)}, u32[]{:S(2)}) async-start(bf16[4,8,16384]{2,1,0:T(8,128)(2,1)} %fusion.1), calls=%async_computation.2 | async-start | bytes 2097152 | tf_op jit(solution)/shard_map/all_to_all | solution.py:89
  56.4 72.0 %all-reduce.2.cloned.1.call-start = ((), (), s32[]{:S(2)}) async-start(), calls=%async_computation.3 | async-start | bytes 1048576 | tf_op jit(solution)/shard_map/psum | solution.py:130
  61.6 22.0 %collective-permute-start.1 = (f32[3,256,20]{2,1,0:T(8,128)S(1)}, f32[3,256,20]{2,1,0:T(8,128)S(1)}, u32[]{:S(2)}, u32[]{:S(2)}) collective-permute-start(f32[3,256,20]{2,1,0:T(8,128)S(1)} %get-tuple-element.7), channel_id=1, source_target_pairs={{4,0},{8,4},{12,8},{5,1},{9,5},{13,9},{6,2},{10,6},{14,10},{7,3},{... | collective-permute-start | bytes 184328 | tf_op jit(solution)/shard_map/ppermute | solution.py:21
  62.9 20.7 %collective-permute-start = (f32[3,256,20]{2,1,0:T(8,128)S(1)}, f32[3,256,20]{2,1,0:T(8,128)S(1)}, u32[]{:S(2)}, u32[]{:S(2)}) collective-permute-start(f32[3,256,20]{2,1,0:T(8,128)S(1)} %get-tuple-element.6), channel_id=1, source_target_pairs={{0,4},{4,8},{8,12},{1,5},{5,9},{9,13},{2,6},{6,10},{10,14},{3,7},{... | collective-permute-start | bytes 184328 | tf_op jit(solution)/shard_map/ppermute | solution.py:18
  83.5 0.9 copy-start.4
  83.6 0.9 copy-start.6
  84.5 9.7 %copy-start.2 = (f32[1,552,512]{2,1,0:T(8,128)S(1)}, f32[1,552,512]{2,1,0:T(8,128)}, u32[]{:S(2)}) copy-start(f32[1,552,512]{2,1,0:T(8,128)} %select_divide_fusion.2) | copy-start | bytes 3391492
  84.5 8.9 %collective-permute-start.3 = (f32[3,20,552]{2,1,0:T(8,128)}, f32[3,20,552]{2,1,0:T(8,128)}, u32[]{:S(2)}, u32[]{:S(2)}) collective-permute-start(f32[3,20,552]{2,1,0:T(8,128)} %get-tuple-element.5), channel_id=1, source_target_pairs={{2,0},{3,1},{6,4},{7,5},{10,8},{11,9},{14,12},{15,13},{18,16},{19,... | collective-permute-start | bytes 397448 | tf_op jit(solution)/shard_map/ppermute | solution.py:21
  85.9 8.2 %collective-permute-start.2 = (f32[3,20,552]{2,1,0:T(8,128)S(1)}, f32[3,20,552]{2,1,0:T(8,128)}, u32[]{:S(2)}, u32[]{:S(2)}) collective-permute-start(f32[3,20,552]{2,1,0:T(8,128)S(1)} %get-tuple-element.4), channel_id=1, source_target_pairs={{0,2},{1,3},{4,6},{5,7},{8,10},{9,11},{12,14},{13,15},{16,18},{17,... | collective-permute-start | bytes 397448 | tf_op jit(solution)/shard_map/ppermute | solution.py:18
  91.8 2.4 %copy-start.5 = (f32[3,256,20]{2,1,0:T(8,128)S(1)}, f32[3,256,20]{2,1,0:T(8,128)}, u32[]{:S(2)}) copy-start(f32[3,256,20]{2,1,0:T(8,128)} %copy-done.4) | copy-start | bytes 184324
  94.2 6.7 %copy-start.1 = (f32[1,296,256]{2,1,0:T(8,128)S(1)}, f32[1,296,256]{2,1,0:T(8,128)}, u32[]{:S(2)}) copy-start(f32[1,296,256]{2,1,0:T(8,128)} %get-tuple-element.15) | copy-start | bytes 909316
Sparse Core Ops, SparseCore 0:
  103.9 24.4 all-reduce.1
where the time goes:
time: 138 us; the launch traced here: 137 us
  waiting for transfers between devices  58 us (42%)
  starting transfers between devices  27.8 us (20%)
  matrix products  17 us (12%)
  other arithmetic  15.7 us (11%)
  between operations  14.2 us (10%)
  local copies, waits for them, and re-layouts  4.37 us (3%)
    psum x1, waiting for transfers between devices, local(): detection = lax.psum(coadded * coadded * denominator, 'band')  24.6 us
    all_to_all x1, waiting for transfers between devices, local(): lax.all_to_all(send_weighted, 'exp', split_axis=0, concat_axis=0, tiled=T...  16.2 us
    ppermute x2, waiting for transfers between devices, extended(): lax.ppermute(lax.slice_in_dim(block, 0, width, axis=dim), axis, backward)  15.4 us
    ppermute x2, starting transfers between devices, extended(): lax.ppermute(lax.slice_in_dim(block, block.shape[dim] - width, None, axis...  10.5 us
    div x4, other arithmetic, band_matrix(): jnp.where(inside, jnp.exp(-offset * offset / (2.0 * spread * spread)), 0.0)  8.28 us
    dot_general x1, matrix products, local(): jnp.einsum('kyp,kpc->kyc', framed, column_mix, precision=lax.Precision.HI...  6.67 us
    all_to_all x1, starting transfers between devices, local(): lax.all_to_all(labels, 'exp', split_axis=0, concat_axis=0, tiled=True)  6.35 us
    all_to_all x1, starting transfers between devices, local(): lax.all_to_all(send_weight, 'exp', split_axis=0, concat_axis=0, tiled=True)  4.26 us
  transfers between devices with their start and end apart: 8, of which 5 were waited for; matrix products, arithmetic and copies ran while one was open for 16% of the time, Pallas kernels for 0%

commit v1 on v0

--- a/solution.py
+++ b/solution.py
@@ -127,7 +127,7 @@
     matched = jnp.einsum("kry,kyc->rc", row_mix, across, precision=lax.Precision.HIGHEST)
     denominator = 1.0 + depth_tile
     coadded = matched / denominator
-    detection = lax.psum(coadded * coadded * denominator, "band")
+    detection = jnp.sum(lax.all_gather(coadded * coadded * denominator, "band"), axis=0)
     return (coadded[None], detection)
 
 

time: 138 us -> 128 us (0.928)
  waiting for transfers between devices: 58 us -> 48.4 us
  other arithmetic: 15.7 us -> 17.9 us
  local copies, waits for them, and re-layouts: 4.37 us -> 2.5 us
    psum x1 -> x0, waiting for transfers between devices: 24.6 us -> none  [local(): detection = lax.psum(coadded * coadded * denominator, 'band')]
    all_gather x0 -> x1, waiting for transfers between devices: none -> 15.1 us  [local(): lax.all_gather(coadded * coadded * denominator, 'band')]
    reduce_sum x0 -> x1, other arithmetic: none -> 2.15 us  [local(): jnp.sum(lax.all_gather(coadded * coadded * denominator, 'band'), axis=0)]
    unnamed x18 -> x17, local copies, waits for them, and re-layouts: 2.69 us -> 0.82 us
  transfers between devices with their start and end apart: 8 -> 8, of which waited for: 5 -> 5; matrix products, arithmetic and copies ran while one was open for 16% -> 17% of each run, Pallas kernels for 0% -> 0%
where the time goes in v1:
time: 128 us
  waiting for transfers between devices  48.4 us (38%)
  starting transfers between devices  27.8 us (22%)
  other arithmetic  17.9 us (14%)
  matrix products  17 us (13%)
  between operations  14.2 us (11%)
  local copies, waits for them, and re-layouts  2.5 us (2%)
    all_to_all x1, waiting for transfers between devices, local(): lax.all_to_all(send_weighted, 'exp', split_axis=0, concat_axis=0, tiled=T...  16.2 us
    ppermute x2, waiting for transfers between devices, extended(): lax.ppermute(lax.slice_in_dim(block, 0, width, axis=dim), axis, backward)  15.4 us
    all_gather x1, waiting for transfers between devices, local(): lax.all_gather(coadded * coadded * denominator, 'band')  15.1 us
    ppermute x2, starting transfers between devices, extended(): lax.ppermute(lax.slice_in_dim(block, block.shape[dim] - width, None, axis...  10.5 us
    div x4, other arithmetic, band_matrix(): jnp.where(inside, jnp.exp(-offset * offset / (2.0 * spread * spread)), 0.0)  8.28 us
    dot_general x1, matrix products, local(): jnp.einsum('kyp,kpc->kyc', framed, column_mix, precision=lax.Precision.HI...  6.67 us
    all_to_all x1, starting transfers between devices, local(): lax.all_to_all(labels, 'exp', split_axis=0, concat_axis=0, tiled=True)  6.35 us
    all_to_all x1, starting transfers between devices, local(): lax.all_to_all(send_weight, 'exp', split_axis=0, concat_axis=0, tiled=True)  4.26 us
  transfers between devices with their start and end apart: 8, of which 5 were waited for; matrix products, arithmetic and copies ran while one was open for 17% of the time, Pallas kernels for 0%

profile of v1, /device:TPU:0, one launch (start us, length us, event | category | flops | bytes accessed | tf_op | source)
XLA Modules:
  0.0 127.9 jit_solution(11652422522278614923)
XLA Ops:
  7.2 0.0 copy-start
  7.2 0.7 add_bitcast_fusion
  7.9 0.9 convert_reduce_fusion
  8.8 0.7 multiply_add_fusion.1
  9.5 0.7 select_reduce_fusion.1
  10.2 0.1 stack.9
  10.3 0.1 sub.118
  10.4 0.6 copy.15
  11.0 6.3 %all-to-all-start = ((s32[4,8,2]{1,2,0:T(2,128)}), s32[4,8,2]{1,2,0:T(2,128)S(1)}, u32[]{:S(2)}, u32[]{:S(2)}) async-start(s32[4,8,2]{1,2,0:T(2,128)} %copy.15), calls=%async_computation | async-start | bytes 8192 | tf_op jit(solution)/shard_map/all_to_all | solution.py:90
  17.4 1.5 %subtract_select_fusion = f32[1,1,16,128,128]{4,3,2,1,0:T(8,128)S(1)} fusion(s32[1,1,16,128,128]{4,3,2,1,0:T(8,128)} %param.8), kind=kLoop, calls=%fused_computation.36 | loop fusion | flops 1835008 | bytes 2097152 | tf_op jit(solution)/shard_map/jit(_where)/select_n | solution.py:29
  18.8 0.0 copy-start.7
  18.8 0.1 convert.1
  18.9 0.5 copy-done.7
  19.5 2.4 %fusion = bf16[4,8,16384]{2,1,0:T(8,128)(2,1)} fusion(f32[2,8,128,128]{3,2,1,0:T(8,128)S(1)} %convert.1, f32[2,8,128,128]{3,2,1,0:T(8,128)S(1)} %bitcast.89, f32[16]{0:T(128)S(1)} %bitcast.97, s32[16]{0:T(128)S(1)} %multiply_add_fusion.1), kind=kOutput, calls=%fused_computation.2 | convolution fusion | flops 18088448 | bytes 3145856 | tf_op jit(solution)/shard_map/dot_general | solution.py:83
  21.9 1.1 all-to-all-done
  22.9 4.0 %all-to-all-start.1 = ((bf16[4,8,16384]{2,1,0:T(8,128)(2,1)}), bf16[4,8,16384]{2,1,0:T(8,128)(2,1)S(1)}, u32[]{:S(2)}, u32[]{:S(2)}) async-start(bf16[4,8,16384]{2,1,0:T(8,128)(2,1)} %fusion), calls=%async_computation.1 | async-start | bytes 2097152 | tf_op jit(solution)/shard_map/all_to_all | solution.py:88
  27.0 0.6 exponential_reduce_fusion
  27.6 0.6 exponential_reduce_fusion.1
  28.2 0.6 exponential_reduce_fusion.2
  28.8 1.8 %fusion.1 = bf16[4,8,16384]{2,1,0:T(8,128)(2,1)} fusion(f32[2,8,128,128]{3,2,1,0:T(8,128)S(1)} %bitcast.90, f32[16]{0:T(128)S(1)} %bitcast.98, s32[16]{0:T(128)S(1)} %multiply_add_fusion.1), kind=kOutput, calls=%fused_computation.3 | convolution fusion | flops 17826304 | bytes 2097280 | tf_op jit(solution)/shard_map/dot_general | solution.py:77
  30.6 2.0 %select_divide_fusion.2 = f32[1,552,512]{2,1,0:T(8,128)} fusion(f32[]{:T(128)} %exponential_reduce_fusion.2), kind=kLoop, calls=%fused_computation.26 | loop fusion | flops 2826240 | bytes 1130500 | tf_op jit(solution)/shard_map/div | solution.py:42
  32.6 3.3 %select_divide_fusion = (f32[1,552,512]{2,1,0:T(8,128)}, f32[1,552,512]{2,1,0:T(8,128)}) fusion(f32[]{:T(128)} %exponential_reduce_fusion, f32[]{:T(128)} %exponential_reduce_fusion.1), kind=kLoop, calls=%fused_computation.24 | loop fusion | flops 3674112 | bytes 2261000 | tf_op jit(solution)/shard_map/div | solution.py:42
  36.0 16.2 %all-to-all-done.1 = bf16[4,8,16384]{2,1,0:T(8,128)(2,1)S(1)} async-done(((bf16[4,8,16384]{2,1,0:T(8,128)(2,1)}), bf16[4,8,16384]{2,1,0:T(8,128)(2,1)S(1)}, u32[]{:S(2)}, u32[]{:S(2)}) %all-to-all-start.1) | async-done | bytes 1048608 | tf_op jit(solution)/shard_map/all_to_all | solution.py:88
  52.1 4.3 %all-to-all-start.2 = ((bf16[4,8,16384]{2,1,0:T(8,128)(2,1)}), bf16[4,8,16384]{2,1,0:T(8,128)(2,1)}, u32[]{:S(2)}, u32[]{:S(2)}) async-start(bf16[4,8,16384]{2,1,0:T(8,128)(2,1)} %fusion.1), calls=%async_computation.2 | async-start | bytes 2097152 | tf_op jit(solution)/shard_map/all_to_all | solution.py:89
  56.4 0.0 all-gather.3.cloned.1.call-start
  56.4 2.2 %select_divide_fusion.3 = (f32[1,296,256]{2,1,0:T(8,128)S(1)}, f32[1,296,256]{2,1,0:T(8,128)}) fusion(f32[]{:T(128)} %exponential_reduce_fusion, f32[]{:T(128)} %exponential_reduce_fusion.1), kind=kLoop, calls=%fused_computation.48 | loop fusion | flops 985088 | bytes 606216 | tf_op jit(solution)/shard_map/div | solution.py:42
  58.6 0.1 reshape.298
  58.7 0.2 convolution_bitcast_fusion.2
  58.9 0.1 compare_convert_fusion
  59.0 0.3 copy.27
  59.3 1.5 %convolution_bitcast_fusion = f32[3,2,128,4,128]{4,3,2,1,0:T(4,128)S(1)} fusion(bf16[128,128,32,1,1]{1,0,2,4,3:T(8,128)(2,1)S(1)} %bitcast.92, f32[2,4,32]{2,1,0:T(4,128)S(1)} %compare_convert_fusion, f32[3,32]{1,0:T(4,128)S(1)} %convolution_bitcast_fusion.2), kind=kOutput, calls=%fused_computation.20 | convolution fusion | flops 150995712 | bytes 2622848 | tf_op jit(solution)/shard_map/kbp,px->kbx/dot_general | solution.py:99
  60.8 0.6 reshape.301
  61.4 0.2 fusion.42
  61.6 1.3 %collective-permute-start.1 = (f32[3,256,20]{2,1,0:T(8,128)S(1)}, f32[3,256,20]{2,1,0:T(8,128)S(1)}, u32[]{:S(2)}, u32[]{:S(2)}) collective-permute-start(f32[3,256,20]{2,1,0:T(8,128)S(1)} %get-tuple-element.7), channel_id=1, source_target_pairs={{4,0},{8,4},{12,8},{5,1},{9,5},{13,9},{6,2},{10,6},{14,10},{7,3},{... | collective-permute-start | bytes 184328 | tf_op jit(solution)/shard_map/ppermute | solution.py:21
  62.9 4.6 %collective-permute-start = (f32[3,256,20]{2,1,0:T(8,128)S(1)}, f32[3,256,20]{2,1,0:T(8,128)S(1)}, u32[]{:S(2)}, u32[]{:S(2)}) collective-permute-start(f32[3,256,20]{2,1,0:T(8,128)S(1)} %get-tuple-element.6), channel_id=1, source_target_pairs={{0,4},{4,8},{8,12},{1,5},{5,9},{9,13},{2,6},{6,10},{10,14},{3,7},{... | collective-permute-start | bytes 184328 | tf_op jit(solution)/shard_map/ppermute | solution.py:18
  67.5 0.7 select_divide_fusion.5
  68.2 15.4 %collective-permute-done.1 = f32[3,256,20]{2,1,0:T(8,128)S(1)} collective-permute-done((f32[3,256,20]{2,1,0:T(8,128)S(1)}, f32[3,256,20]{2,1,0:T(8,128)S(1)}, u32[]{:S(2)}, u32[]{:S(2)}) %collective-permute-start.1) | collective-permute-done | bytes 61472 | tf_op jit(solution)/shard_map/ppermute | solution.py:21
  83.6 0.0 collective-permute-done
  83.6 0.9 pad_maximum_fusion.2
  84.5 1.4 %collective-permute-start.3 = (f32[3,20,552]{2,1,0:T(8,128)}, f32[3,20,552]{2,1,0:T(8,128)}, u32[]{:S(2)}, u32[]{:S(2)}) collective-permute-start(f32[3,20,552]{2,1,0:T(8,128)} %get-tuple-element.5), channel_id=1, source_target_pairs={{2,0},{3,1},{6,4},{7,5},{10,8},{11,9},{14,12},{15,13},{18,16},{19,... | collective-permute-start | bytes 397448 | tf_op jit(solution)/shard_map/ppermute | solution.py:21
  85.9 5.9 %collective-permute-start.2 = (f32[3,20,552]{2,1,0:T(8,128)S(1)}, f32[3,20,552]{2,1,0:T(8,128)}, u32[]{:S(2)}, u32[]{:S(2)}) collective-permute-start(f32[3,20,552]{2,1,0:T(8,128)S(1)} %get-tuple-element.4), channel_id=1, source_target_pairs={{0,2},{1,3},{4,6},{5,7},{8,10},{9,11},{12,14},{13,15},{16,18},{17,... | collective-permute-start | bytes 397448 | tf_op jit(solution)/shard_map/ppermute | solution.py:18
  91.8 1.6 %convolution_add_fusion = f32[2,4,128,128]{3,1,2,0:T(4,128)S(1)} fusion(s32[32]{0:T(128)S(1)} %get-tuple-element.9, s32[2,4]{1,0:T(2,128)S(1)} %multiply_add_fusion, bf16[4,8,16384]{2,1,0:T(8,128)(2,1)} %all-to-all-done.2), kind=kOutput, calls=%fused_computation.22 | convolution fusion | flops 8519936 | bytes 1573024 | tf_op jit(solution)/shard_map/dot_general | solution.py:105
  93.4 0.7 collective-permute-done.2
  94.2 6.7 %fusion.2 = f32[3,296,512]{2,1,0:T(8,128)S(1)} fusion(f32[1,552,512]{2,1,0:T(8,128)} %get-tuple-element.12, f32[1,552,512]{2,1,0:T(8,128)} %get-tuple-element.13, f32[1,552,512]{2,1,0:T(8,128)S(1)} %copy-done.2, f32[3,20,552]{2,1,0:T(8,128)} %collective-permute-done.3, f32[3,256,20]{2,1,0:T(8,128)S(1)} %copy-done.5, f32[3,256,512]{2,1,0:T(8,128)S(1)} %reshape.301, ...), kind=kOutput, calls=%fused_computation.4 | convolution fusion | flops 3015297792 | bytes 7170816 | tf_op jit(solution)/shard_map/kyp,kpc->kyc/dot_general | solution.py:126
  100.8 2.9 %bitcast_multiply_fusion.2 = (f32[256,512]{1,0:T(8,128)}, f32[256,512]{1,0:T(8,128)}) fusion(f32[32,8,4,128]{3,2,1,0:T(4,128)S(1)} %bitcast.93, f32[3,296,512]{2,1,0:T(8,128)S(1)} %fusion.2, f32[1,296,256]{2,1,0:T(8,128)S(1)} %get-tuple-element.14, f32[1,296,256]{2,1,0:T(8,128)S(1)} %copy-done.1, f32[1,296,256]{2,1,0:T(8,128)S(1)} %select_divide_fusion.5), kind=kOutput, calls=%fused_computation.44 | convolution fusion | flops 1397551104 | bytes 4300800 | tf_op jit(solution)/shard_map/kry,kyc->rc/dot_general | solution.py:127
  103.8 0.0 all-gather.3.cloned.1.call-update
  103.8 15.1 %all-gather.3.cloned.1.call-done = f32[512,512]{1,0:T(8,128)} async-done(((f32[256,512]{1,0:T(8,128)}), f32[512,512]{1,0:T(8,128)}) %all-gather.3.cloned.1.call-update) | async-done | bytes 1048592 | tf_op jit(solution)/shard_map/all_gather | solution.py:130
  118.9 2.1 %reduce_sum.81 = f32[256,512]{1,0:T(8,128)} reduce(f32[2,256,512]{2,1,0:T(8,128)} %bitcast.94, f32[]{:T(128)} %constant.19.clone.1), dimensions={0}, to_apply=%region_6.7 | reduce | flops 131072 | bytes 1572868 | tf_op jit(solution)/shard_map/reduce_sum | solution.py:130
  (20 shorter events, 0.1 us)
Async XLA Ops:
  7.2 51.6 %copy-start = (f32[64,3]{0,1:T(4,128)S(1)}, f32[64,3]{0,1:T(4,128)}, u32[]{:S(2)}) copy-start(f32[64,3]{0,1:T(4,128)} %param.13) | copy-start | bytes 2308
  7.2 11.7 %copy-start.3 = (bf16[1,1,16,128,128]{4,3,2,1,0:T(8,128)(2,1)S(1)}, bf16[1,1,16,128,128]{4,3,2,1,0:T(8,128)(2,1)}, u32[]{:S(2)}) copy-start(bf16[1,1,16,128,128]{4,3,2,1,0:T(8,128)(2,1)} %param.7) | copy-start | bytes 1572868
  11.0 11.9 %all-to-all-start = ((s32[4,8,2]{1,2,0:T(2,128)}), s32[4,8,2]{1,2,0:T(2,128)S(1)}, u32[]{:S(2)}, u32[]{:S(2)}) async-start(s32[4,8,2]{1,2,0:T(2,128)} %copy.15), calls=%async_computation | async-start | bytes 8192 | tf_op jit(solution)/shard_map/all_to_all | solution.py:90
  18.8 0.7 copy-start.7
  22.9 29.2 %all-to-all-start.1 = ((bf16[4,8,16384]{2,1,0:T(8,128)(2,1)}), bf16[4,8,16384]{2,1,0:T(8,128)(2,1)S(1)}, u32[]{:S(2)}, u32[]{:S(2)}) async-start(bf16[4,8,16384]{2,1,0:T(8,128)(2,1)} %fusion), calls=%async_computation.1 | async-start | bytes 2097152 | tf_op jit(solution)/shard_map/all_to_all | solution.py:88
  52.1 39.7 %all-to-all-start.2 = ((bf16[4,8,16384]{2,1,0:T(8,128)(2,1)}), bf16[4,8,16384]{2,1,0:T(8,128)(2,1)}, u32[]{:S(2)}, u32[]{:S(2)}) async-start(bf16[4,8,16384]{2,1,0:T(8,128)(2,1)} %fusion.1), calls=%async_computation.2 | async-start | bytes 2097152 | tf_op jit(solution)/shard_map/all_to_all | solution.py:89
  56.4 62.5 %all-gather.3.cloned.1.call-start = ((), (), s32[]{:S(2)}) async-start(), calls=%async_computation.3 | async-start | bytes 1572864 | tf_op jit(solution)/shard_map/all_gather | solution.py:130
  61.6 22.0 %collective-permute-start.1 = (f32[3,256,20]{2,1,0:T(8,128)S(1)}, f32[3,256,20]{2,1,0:T(8,128)S(1)}, u32[]{:S(2)}, u32[]{:S(2)}) collective-permute-start(f32[3,256,20]{2,1,0:T(8,128)S(1)} %get-tuple-element.7), channel_id=1, source_target_pairs={{4,0},{8,4},{12,8},{5,1},{9,5},{13,9},{6,2},{10,6},{14,10},{7,3},{... | collective-permute-start | bytes 184328 | tf_op jit(solution)/shard_map/ppermute | solution.py:21
  62.9 20.7 %collective-permute-start = (f32[3,256,20]{2,1,0:T(8,128)S(1)}, f32[3,256,20]{2,1,0:T(8,128)S(1)}, u32[]{:S(2)}, u32[]{:S(2)}) collective-permute-start(f32[3,256,20]{2,1,0:T(8,128)S(1)} %get-tuple-element.6), channel_id=1, source_target_pairs={{0,4},{4,8},{8,12},{1,5},{5,9},{9,13},{2,6},{6,10},{10,14},{3,7},{... | collective-permute-start | bytes 184328 | tf_op jit(solution)/shard_map/ppermute | solution.py:18
  83.5 0.9 copy-start.4
  83.6 0.9 copy-start.6
  84.5 9.7 %copy-start.2 = (f32[1,552,512]{2,1,0:T(8,128)S(1)}, f32[1,552,512]{2,1,0:T(8,128)}, u32[]{:S(2)}) copy-start(f32[1,552,512]{2,1,0:T(8,128)} %select_divide_fusion.2) | copy-start | bytes 3391492
  84.5 8.9 %collective-permute-start.3 = (f32[3,20,552]{2,1,0:T(8,128)}, f32[3,20,552]{2,1,0:T(8,128)}, u32[]{:S(2)}, u32[]{:S(2)}) collective-permute-start(f32[3,20,552]{2,1,0:T(8,128)} %get-tuple-element.5), channel_id=1, source_target_pairs={{2,0},{3,1},{6,4},{7,5},{10,8},{11,9},{14,12},{15,13},{18,16},{19,... | collective-permute-start | bytes 397448 | tf_op jit(solution)/shard_map/ppermute | solution.py:21
  85.9 8.2 %collective-permute-start.2 = (f32[3,20,552]{2,1,0:T(8,128)S(1)}, f32[3,20,552]{2,1,0:T(8,128)}, u32[]{:S(2)}, u32[]{:S(2)}) collective-permute-start(f32[3,20,552]{2,1,0:T(8,128)S(1)} %get-tuple-element.4), channel_id=1, source_target_pairs={{0,2},{1,3},{4,6},{5,7},{8,10},{9,11},{12,14},{13,15},{16,18},{17,... | collective-permute-start | bytes 397448 | tf_op jit(solution)/shard_map/ppermute | solution.py:18
  91.8 2.4 %copy-start.5 = (f32[3,256,20]{2,1,0:T(8,128)S(1)}, f32[3,256,20]{2,1,0:T(8,128)}, u32[]{:S(2)}) copy-start(f32[3,256,20]{2,1,0:T(8,128)} %copy-done.4) | copy-start | bytes 184324
  94.2 6.7 %copy-start.1 = (f32[1,296,256]{2,1,0:T(8,128)S(1)}, f32[1,296,256]{2,1,0:T(8,128)}, u32[]{:S(2)}) copy-start(f32[1,296,256]{2,1,0:T(8,128)} %get-tuple-element.15) | copy-start | bytes 909316
Sparse Core Ops, SparseCore 0:
  103.9 14.8 all-gather.2
